TPU v7x, 32 devices: a whole 2x2x4 slice. The times are simulated.
32 devices in a mesh: groups: 2 (over y), req: 8 (over z, core), head: 2 (over x), rep: 1.
Axes of the slice: x: 2, y: 2, z: 4, core: 2. Of those that a mesh axis runs over, the one named last changes fastest.
Arguments:
- candidates: bfloat16 [32768, 1024], P(('groups', 'req', 'rep')), parts along dimension 0, may hold values from -6 to 6
- candidate_request: int32 [16, 2048], P(('groups', 'req'), 'rep'), parts along dimension 0, may hold values from 0 to 7, never falling along the last dimension, each value on 1 to 512 neighbouring positions
- request_owner: int32 [128, 1], P(('groups', 'req')), parts along dimension 0, may hold values from 0 to 7; in each aligned block of 8 rows (0 to 7, 8 to 15, ...) no two rows name the same one
- request_user: int32 [128], P(('groups', 'req')), parts along dimension 0, may hold values from 0 to 7
- request_blocks: int32 [16, 8], P(('groups', 'req')), parts along dimension 0, may hold values from 1 to 4, 24 in all within a row
- kv_cache: bfloat16 [128, 512, 2048], P(('groups', 'req'), None, 'head'), parts along dimension 0, may hold values from -6 to 6
- w_in: bfloat16 [1024, 4096], P(None, 'head'), may hold values from -0.1875 to 0.1875
- w_out: bfloat16 [1024, 1024], P('head'), may hold values from -0.1875 to 0.1875
Outputs:
- ranked: bfloat16 [32768, 1024], P(('groups', 'req', 'rep'), 'head'), parts along dimension 0
There are 2 independent parts, one for each index of `groups`. A program takes and returns all parts, laid end to end along the dimension named above; an argument that names none is the same for every part. Nothing has to cross between parts.
Inputs may be any that keep to these rules, and one draw needn't show every extreme that they name: `request_owner`: among the 8 requests of one req index at most 1 name the same owner, a bound that some block reaches of them. `request_blocks`: the 8 lengths of one req index sum to 24; some request has 4. `candidate_request`: never falls along the 2048 candidates of one req index; every request has 1 to 512 candidates, one exactly 512.
All inputs are finite; a program needn't handle non-finite values.
Results may differ from a plain program's by a relative error of at most 0.0056.
Values may be sent and summed in bfloat16 or wider, within the bound.
A program may use at most 128 MiB of HBM per device.

v0:
```python
import math
import jax
import jax.numpy as jnp
from jax import lax
from jax.sharding import PartitionSpec as P

HD = 128
BLOCK = 128
CAP = 1
MOSTC = 512
EPSILON = 1e-05


def normalize(values):
    center = values - jnp.mean(values, axis=-1, keepdims=True)
    spread = jnp.mean(center * center, axis=-1, keepdims=True)
    return center * lax.rsqrt(spread + EPSILON)


def slot_ranks(owner_rows):
    width = owner_rows.shape[-1]
    same_owner = owner_rows[..., :, None] == owner_rows[..., None, :]
    earlier = jnp.arange(width)[None, :] < jnp.arange(width)[:, None]
    return jnp.sum(jnp.logical_and(same_owner, earlier).astype(jnp.int32), axis=-1)


def per_device(
    candidates,
    candidate_request,
    request_owner,
    request_user,
    request_blocks,
    kv_cache,
    w_in,
    w_out,
):
    shard_rows = candidates.shape[0]
    local_heads = w_out.shape[0] // HD
    req_count = lax.axis_size("req")
    myself = lax.axis_index("req")
    owners = request_owner[:, 0]
    lengths = request_blocks[0]
    all_owners, all_users = (
        lax.all_gather(owners, "req", axis=0, tiled=True),
        lax.all_gather(request_user, "req", axis=0, tiled=True),
    )
    all_owners = all_owners.reshape(req_count, -1)
    all_users = all_users.reshape(req_count, -1)
    ranks_all = slot_ranks(all_owners)
    slot_ids = jnp.arange(CAP)
    chosen = jnp.logical_and(
        (all_owners == myself)[:, None, :], ranks_all[:, None, :] == slot_ids[None, :, None]
    )
    chosen_int = chosen.astype(jnp.int32)
    present = jnp.sum(chosen_int, axis=-1) > 0
    user_slot = jnp.sum(chosen_int * all_users[:, None, :], axis=-1)
    picked = kv_cache[user_slot]
    arrived = lax.all_to_all(
        jnp.where(present[:, :, None, None], picked, jnp.zeros_like(picked)),
        "req",
        split_axis=0,
        concat_axis=0,
        tiled=True,
    )
    own_ranks = slot_ranks(owners)
    normed = normalize(candidates.astype(jnp.float32)).astype(jnp.bfloat16)
    projected = jax.nn.silu(jnp.dot(normed, w_in, preferred_element_type=jnp.float32)).astype(
        jnp.bfloat16
    )
    projected = projected.reshape(shard_rows, local_heads, 4, HD)
    gates = projected[:, :, 0]
    values_own = projected[:, :, 1]
    queries = projected[:, :, 2]
    keys_own = projected[:, :, 3]
    scale = 1.0 / math.sqrt(HD)
    self_score = (
        jnp.sum(queries.astype(jnp.float32) * keys_own.astype(jnp.float32), axis=-1) * scale
    )
    attended = jax.nn.silu(self_score)[..., None] * values_own.astype(jnp.float32)
    segment = candidate_request[0]
    window = min(MOSTC, shard_rows)
    token_pos = jnp.arange(arrived.shape[2])

    def add_request(request, total):
        start = jnp.sum((segment < request).astype(jnp.int32))
        start = jnp.clip(start, 0, shard_rows - window)
        rows_q = lax.dynamic_slice_in_dim(queries, start, window, 0)
        rows_seg = lax.dynamic_slice_in_dim(segment, start, window, 0)
        source = owners[request]
        slot = own_ranks[request]
        cached = arrived[source, slot].reshape(-1, local_heads, 2, HD)
        live = token_pos < lengths[request] * BLOCK
        scores = (
            jnp.einsum("whd,thd->hwt", rows_q, cached[:, :, 0], preferred_element_type=jnp.float32)
            * scale
        )
        weights = jnp.where(live[None, None, :], jax.nn.silu(scores), 0.0).astype(jnp.bfloat16)
        mixed = jnp.einsum(
            "hwt,thd->whd", weights, cached[:, :, 1], preferred_element_type=jnp.float32
        )
        mixed = jnp.where((rows_seg == request)[:, None, None], mixed, 0.0)
        current = lax.dynamic_slice_in_dim(total, start, window, 0)
        return lax.dynamic_update_slice_in_dim(total, current + mixed, start, 0)

    attended = lax.fori_loop(0, owners.shape[0], add_request, attended)
    gated = (
        (normalize(attended) * gates.astype(jnp.float32))
        .astype(jnp.bfloat16)
        .reshape(shard_rows, -1)
    )
    partial_out = jnp.dot(gated, w_out, preferred_element_type=jnp.float32)
    summed = lax.psum_scatter(partial_out, "head", scatter_dimension=1, tiled=True)
    columns = summed.shape[1]
    residual = lax.dynamic_slice_in_dim(
        candidates, lax.axis_index("head") * columns, columns, 1
    ).astype(jnp.float32)
    return (summed + residual).astype(jnp.bfloat16)


def solution(mesh):
    placed = (
        P(("groups", "req", "rep"), None),
        P(("groups", "req"), "rep"),
        P(("groups", "req"), None),
        P(("groups", "req")),
        P(("groups", "req"), None),
        P(("groups", "req"), None, "head"),
        P(None, "head"),
        P("head", None),
    )
    return jax.shard_map(
        per_device,
        mesh=mesh,
        in_specs=placed,
        out_specs=P(("groups", "req", "rep"), "head"),
        check_vma=False,
    )
```

profile of v0, /device:TPU:0, one launch (start us, length us, event | category | flops | bytes accessed | tf_op | source)
XLA Modules:
  0.0 481.6 jit_solution(14917906185347774815)
XLA Ops:
  6.5 1.3 dynamic-slice
  8.5 0.8 bitcast_dynamic-update-slice_fusion
  9.3 0.8 dynamic-update-slice.1
  10.1 10.6 %all-reduce.2 = (s32[64]{0:T(128)S(1)}, s32[64]{0:T(128)S(1)}) all-reduce(s32[64]{0:T(128)S(1)} %bitcast_dynamic-update-slice_fusion, s32[64]{0:T(128)S(1)} %dynamic-update-slice.1), channel_id=2, replica_groups=mesh['groups'=2,'req'=8,'head'=2,'rep'=1] {'req'}, use_global_device_ids=true, to_apply=%add | all-reduce | flops 128 | bytes 1024
  21.5 8.1 %gather_fusion = bf16[8,512,1024]{2,1,0:T(8,128)(2,1)} fusion(bf16[8,512,1024]{2,1,0:T(8,128)(2,1)} %param.15, s32[1024]{0:T(1024)S(1)} %pad_clamp_fusion), kind=kCustom, calls=%fused_computation | custom fusion | bytes 16777248 | tf_op jit(solution)/shard_map/gather | solution.py:57
  29.6 7.2 %fusion.17 = bf16[8,1,512,1024]{3,2,1,0:T(8,128)(2,1)} fusion(bf16[8,512,1024]{2,1,0:T(8,128)(2,1)} %gather_fusion, pred[8]{0:T(512)(128)(4,1)S(1)} %broadcast_compare_fusion.1), kind=kLoop, calls=%fused_computation.26 | loop fusion | flops 4194304 | bytes 16777224 | tf_op jit(solution)/shard_map/jit(_where)/select_n | solution.py:59
  36.8 5.0 %all-to-all-start = ((bf16[8,1,512,1024]{3,2,1,0:T(8,128)(2,1)}), bf16[8,1,512,1024]{3,2,1,0:T(8,128)(2,1)}, u32[]{:S(2)}, u32[]{:S(2)}) async-start(bf16[8,1,512,1024]{3,2,1,0:T(8,128)(2,1)} %fusion.17), calls=%async_computation | async-start | bytes 16777216 | tf_op jit(solution)/shard_map/all_to_all | solution.py:58
  42.1 3.0 convert_reduce_fusion.1
  45.5 1.4 fusion.15
  46.9 15.4 %multiply_convert_fusion = bf16[2048,2048]{0,1:T(8,128)(2,1)S(1)} fusion(bf16[1024,2048]{1,0:T(8,128)(2,1)} %param.16, bf16[2048,1024]{1,0:T(8,128)(2,1)S(1)} %copy-done.2, f32[2048]{0:T(1024)S(1)} %add_rsqrt_fusion.1, f32[2048]{0:T(1024)S(1)} %broadcast_multiply_fusion.1), kind=kOutput, calls=%fused_computation.18 | convolution fusion | flops 8619294720 | bytes 16793600 | tf_op jit(solution)/shard_map/dot_general | solution.py:67
  62.4 2.1 fusion.27
  64.4 1.8 copy-done.3
  66.2 2.5 copy.46
  68.7 3.0 copy.47
  71.8 2.8 fusion.21
  74.6 4.2 convert_multiply_fusion.1
  78.7 146.9 %all-to-all-done = bf16[8,1,512,1024]{3,2,1,0:T(8,128)(2,1)} async-done(((bf16[8,1,512,1024]{3,2,1,0:T(8,128)(2,1)}), bf16[8,1,512,1024]{3,2,1,0:T(8,128)(2,1)}, u32[]{:S(2)}, u32[]{:S(2)}) %all-to-all-start) | async-done | bytes 8388640 | tf_op jit(solution)/shard_map/all_to_all | solution.py:58
  225.7 130.5 %while.14 = (s32[]{:T(128)}, f32[2048,4,128]{0,2,1:T(8,128)}, s32[2048]{0:T(1024)S(1)}, s32[8]{0:T(128)S(1)}, bf16[8,1,512,1024]{3,2,1,0:T(8,128)(2,1)}, /*index...) while((s32[]{:T(128)}, f32[2048,4,128]{0,2,1:T(8,128)}, ...), condition=%wide.region_8.9_spmd.clone, body=%wide.region_6.8_spmd.clone.sunk | while | flops 544742400 | bytes 9975023 | solution.py:105
  228.2 1.3 constant_dynamic-slice_fusion.2
  232.7 3.4 fusion.35
  236.2 5.8 %dynamic_update_slice.9 = f32[2048,4,128]{0,2,1:T(8,128)} dynamic-update-slice(f32[2048,4,128]{0,2,1:T(8,128)} %get-tuple-element.275, f32[512,4,128]{0,2,1:T(8,128)S(1)} %fusion.35, s32[]{:T(128)S(6)} %min.10, s32[]{:T(128)} %constant.90.clone.1..sunk, s32[]{:T(128)} %constant.90.clone.1..sunk) | dynamic-update-slice | bytes 2097156 | tf_op jit(solution)/shard_map/while/body/eval_jaxpr/dynamic_update_slice | solution.py:103
  244.5 1.3 constant_dynamic-slice_fusion.2
  248.9 3.4 fusion.35
  252.4 6.3 %dynamic_update_slice.9 = f32[2048,4,128]{0,2,1:T(8,128)} dynamic-update-slice(f32[2048,4,128]{0,2,1:T(8,128)} %get-tuple-element.275, f32[512,4,128]{0,2,1:T(8,128)S(1)} %fusion.35, s32[]{:T(128)S(6)} %min.10, s32[]{:T(128)} %constant.90.clone.1..sunk, s32[]{:T(128)} %constant.90.clone.1..sunk) | dynamic-update-slice | bytes 2097156 | tf_op jit(solution)/shard_map/while/body/eval_jaxpr/dynamic_update_slice | solution.py:103
  261.2 1.3 constant_dynamic-slice_fusion.2
  265.7 3.4 fusion.35
  269.1 6.3 %dynamic_update_slice.9 = f32[2048,4,128]{0,2,1:T(8,128)} dynamic-update-slice(f32[2048,4,128]{0,2,1:T(8,128)} %get-tuple-element.275, f32[512,4,128]{0,2,1:T(8,128)S(1)} %fusion.35, s32[]{:T(128)S(6)} %min.10, s32[]{:T(128)} %constant.90.clone.1..sunk, s32[]{:T(128)} %constant.90.clone.1..sunk) | dynamic-update-slice | bytes 2097156 | tf_op jit(solution)/shard_map/while/body/eval_jaxpr/dynamic_update_slice | solution.py:103
  277.9 1.3 constant_dynamic-slice_fusion.2
  282.4 3.4 fusion.35
  285.8 6.3 %dynamic_update_slice.9 = f32[2048,4,128]{0,2,1:T(8,128)} dynamic-update-slice(f32[2048,4,128]{0,2,1:T(8,128)} %get-tuple-element.275, f32[512,4,128]{0,2,1:T(8,128)S(1)} %fusion.35, s32[]{:T(128)S(6)} %min.10, s32[]{:T(128)} %constant.90.clone.1..sunk, s32[]{:T(128)} %constant.90.clone.1..sunk) | dynamic-update-slice | bytes 2097156 | tf_op jit(solution)/shard_map/while/body/eval_jaxpr/dynamic_update_slice | solution.py:103
  294.6 1.3 constant_dynamic-slice_fusion.2
  299.1 3.4 fusion.35
  302.6 6.3 %dynamic_update_slice.9 = f32[2048,4,128]{0,2,1:T(8,128)} dynamic-update-slice(f32[2048,4,128]{0,2,1:T(8,128)} %get-tuple-element.275, f32[512,4,128]{0,2,1:T(8,128)S(1)} %fusion.35, s32[]{:T(128)S(6)} %min.10, s32[]{:T(128)} %constant.90.clone.1..sunk, s32[]{:T(128)} %constant.90.clone.1..sunk) | dynamic-update-slice | bytes 2097156 | tf_op jit(solution)/shard_map/while/body/eval_jaxpr/dynamic_update_slice | solution.py:103
  311.3 1.3 constant_dynamic-slice_fusion.2
  315.8 3.4 fusion.35
  319.3 6.3 %dynamic_update_slice.9 = f32[2048,4,128]{0,2,1:T(8,128)} dynamic-update-slice(f32[2048,4,128]{0,2,1:T(8,128)} %get-tuple-element.275, f32[512,4,128]{0,2,1:T(8,128)S(1)} %fusion.35, s32[]{:T(128)S(6)} %min.10, s32[]{:T(128)} %constant.90.clone.1..sunk, s32[]{:T(128)} %constant.90.clone.1..sunk) | dynamic-update-slice | bytes 2097156 | tf_op jit(solution)/shard_map/while/body/eval_jaxpr/dynamic_update_slice | solution.py:103
  328.0 1.3 constant_dynamic-slice_fusion.2
  332.5 3.4 fusion.35
  335.9 5.0 %dynamic_update_slice.9 = f32[2048,4,128]{0,2,1:T(8,128)} dynamic-update-slice(f32[2048,4,128]{0,2,1:T(8,128)} %get-tuple-element.275, f32[512,4,128]{0,2,1:T(8,128)S(1)} %fusion.35, s32[]{:T(128)S(6)} %min.10, s32[]{:T(128)} %constant.90.clone.1..sunk, s32[]{:T(128)} %constant.90.clone.1..sunk) | dynamic-update-slice | bytes 2097156 | tf_op jit(solution)/shard_map/while/body/eval_jaxpr/dynamic_update_slice | solution.py:103
  343.4 1.3 constant_dynamic-slice_fusion.2
  347.8 3.3 fusion.35
  351.2 5.0 %dynamic_update_slice.9 = f32[2048,4,128]{0,2,1:T(8,128)} dynamic-update-slice(f32[2048,4,128]{0,2,1:T(8,128)} %get-tuple-element.275, f32[512,4,128]{0,2,1:T(8,128)S(1)} %fusion.35, s32[]{:T(128)S(6)} %min.10, s32[]{:T(128)} %constant.90.clone.1..sunk, s32[]{:T(128)} %constant.90.clone.1..sunk) | dynamic-update-slice | bytes 2097156 | tf_op jit(solution)/shard_map/while/body/eval_jaxpr/dynamic_update_slice | solution.py:103
  356.2 2.5 reduce_sum.98
  358.7 2.9 multiply_reduce_fusion
  362.1 2.4 fusion.20
  364.6 5.6 %fusion.28 = f32[2048,1024]{1,0:T(8,128)} fusion(bf16[2048,512]{0,1:T(8,128)(2,1)S(1)} %bitcast.74, bf16[512,1024]{1,0:T(8,128)(2,1)S(1)} %copy-done), kind=kOutput, calls=%fused_computation.56 | convolution fusion | flops 2147483648 | bytes 11534336 | tf_op jit(solution)/shard_map/dot_general | solution.py:111
  370.2 99.7 %reduce-scatter.2.cloned.1.call-done = f32[2048,512]{1,0:T(8,128)} async-done(((f32[2048,1024]{1,0:T(8,128)}), f32[2048,512]{1,0:T(8,128)}) %reduce-scatter.2.cloned.1.call-update) | async-done | bytes 4194320 | tf_op jit(solution)/shard_map/reduce_scatter | solution.py:112
  469.9 4.9 %add_convert_fusion = bf16[2048,512]{1,0:T(8,128)(2,1)} fusion(f32[2048,512]{1,0:T(8,128)} %reduce-scatter.2.cloned.1.call-done, bf16[2048,1024]{1,0:T(8,128)(2,1)} %param.10, s32[]{:T(128)S(6)} %select_n.71), kind=kLoop, calls=%fused_computation.33 | loop fusion | flops 3145728 | bytes 8388612 | tf_op jit(solution)/shard_map/convert_element_type | solution.py:117
  (72 shorter events, 21.5 us)
Async XLA Ops:
  6.5 358.0 %copy-start = (bf16[512,1024]{1,0:T(8,128)(2,1)S(1)}, bf16[512,1024]{1,0:T(8,128)(2,1)}, u32[]{:S(2)}) copy-start(bf16[512,1024]{1,0:T(8,128)(2,1)} %param.17) | copy-start | bytes 3145732
  36.8 188.9 %all-to-all-start = ((bf16[8,1,512,1024]{3,2,1,0:T(8,128)(2,1)}), bf16[8,1,512,1024]{3,2,1,0:T(8,128)(2,1)}, u32[]{:S(2)}, u32[]{:S(2)}) async-start(bf16[8,1,512,1024]{3,2,1,0:T(8,128)(2,1)} %fusion.17), calls=%async_computation | async-start | bytes 16777216 | tf_op jit(solution)/shard_map/all_to_all | solution.py:58
  41.8 428.0 %reduce-scatter.2.cloned.1.call-start = ((), (), s32[]{:S(2)}) async-start(), calls=%async_computation.2 | async-start | bytes 12582912 | tf_op jit(solution)/shard_map/reduce_scatter | solution.py:112
  42.1 3.5 copy-start.2
  62.4 3.8 copy-start.3
  74.5 151.2 %copy-start.4 = (s32[1,2048]{1,0:T(1,128)S(1)}, s32[1,2048]{1,0:T(1,128)}, u32[]{:S(2)}) copy-start(s32[1,2048]{1,0:T(1,128)} %param.11) | copy-start | bytes 24580
  74.5 151.2 %copy-start.5 = (s32[8,1]{0,1:T(1,128)S(1)}, s32[8,1]{0,1:T(1,128)}, u32[]{:S(2)}) copy-start(s32[8,1]{0,1:T(1,128)} %param.12) | copy-start | bytes 100
  74.5 151.1 %copy-start.6 = (s32[1,8]{1,0:T(1,128)S(1)}, s32[1,8]{1,0:T(1,128)}, u32[]{:S(2)}) copy-start(s32[1,8]{1,0:T(1,128)} %param.14) | copy-start | bytes 100
  358.7 3.5 copy-start.1
Sparse Core Ops, SparseCore 0:
  370.3 99.4 reduce-scatter.1
where the time goes:
time: 484 us; the launch traced here: 482 us
  waiting for transfers between devices  247 us (51%)
  local copies, waits for them, and re-layouts  92.8 us (19%)
  matrix products  48.4 us (10%)
  other arithmetic  37.5 us (8%)
  loops' own time  26.2 us (5%)
  between operations  14.2 us (3%)
  blocking collectives  10.6 us (2%)
  starting transfers between devices  5.26 us (1%)
    all_to_all x1, waiting for transfers between devices, per_device(): lax.all_to_all(jnp.where(present[:, :, None, None], picked, jnp.zeros_lik...  147 us
    reduce_scatter x1, waiting for transfers between devices, per_device(): lax.psum_scatter(partial_out, 'head', scatter_dimension=1, tiled=True)  99.7 us
    dynamic_update_slice x8, local copies, waits for them, and re-layouts, add_request(): return lax.dynamic_update_slice_in_dim(total, current + mixed, start, 0)  47.1 us
    dot_general x8, matrix products, add_request(): jnp.einsum('hwt,thd->whd', weights, cached[:, :, 1], preferred_element_ty...  27.4 us
    another operation x1, loops' own time, per_device(): attended = lax.fori_loop(0, owners.shape[0], add_request, attended)  26.2 us
    dot_general x1, matrix products, per_device(): jnp.dot(normed, w_in, preferred_element_type=jnp.float32)  15.4 us
    dynamic_slice x16, local copies, waits for them, and re-layouts, add_request(): cached = arrived[source, slot].reshape(-1, local_heads, 2, HD)  14.7 us
    unnamed x21, local copies, waits for them, and re-layouts  11.2 us
  transfers between devices with their start and end apart: 2, of which 2 were waited for; matrix products, arithmetic and copies ran while one was open for 7% of the time, Pallas kernels for 0%

commit v1 on v0

--- a/solution.py
+++ b/solution.py
@@ -9,6 +9,18 @@
 CAP = 1
 MOSTC = 512
 EPSILON = 1e-05
+
+
+def cut_along(x, dim, peers):
+    shape = x.shape
+    tiles = x.reshape(*shape[:dim], peers, shape[dim] // peers, *shape[dim + 1 :])
+    return jnp.moveaxis(tiles, dim, 0)
+
+
+def joined_along(parts, dim):
+    shape = list(parts.shape[1:])
+    shape[dim] *= parts.shape[0]
+    return jnp.moveaxis(parts, 0, dim).reshape(shape)
 
 
 def normalize(values):
@@ -55,13 +67,15 @@
     present = jnp.sum(chosen_int, axis=-1) > 0
     user_slot = jnp.sum(chosen_int * all_users[:, None, :], axis=-1)
     picked = kv_cache[user_slot]
-    arrived = lax.all_to_all(
-        jnp.where(present[:, :, None, None], picked, jnp.zeros_like(picked)),
-        "req",
-        split_axis=0,
-        concat_axis=0,
-        tiled=True,
-    )
+    array = jnp.where(present[:, :, None, None], picked, jnp.zeros_like(picked))
+    size, place = (lax.axis_size("req"), lax.axis_index("req"))
+    pieces = cut_along(array, 0, size)
+    gathered = [pieces[place]]
+    for step in range(1, size):
+        sent = pieces[(place + step) % size]
+        gathered.append(lax.ppermute(sent, "req", [(i, (i + step) % size) for i in range(size)]))
+    pieces = jnp.stack(gathered)[(place - jnp.arange(size)) % size]
+    arrived = joined_along(pieces, 0)
     own_ranks = slot_ranks(owners)
     normed = normalize(candidates.astype(jnp.float32)).astype(jnp.bfloat16)
     projected = jax.nn.silu(jnp.dot(normed, w_in, preferred_element_type=jnp.float32)).astype(

time: 484 us -> 493 us (1.019)
  local copies, waits for them, and re-layouts: 92.8 us -> 122 us
  waiting for transfers between devices: 247 us -> 226 us
    all_to_all x1 -> x0, waiting for transfers between devices: 147 us -> none  [per_device(): lax.all_to_all(jnp.where(present[:, :, None, None], picked, jnp.zeros_lik...]
    ppermute x0 -> x7, waiting for transfers between devices: none -> 77.4 us  [per_device(): lax.ppermute(sent, 'req', [(i, (i + step) % size) for i in range(size)])]
    reduce_scatter x1, waiting for transfers between devices: 99.7 us -> 148 us  [per_device(): lax.psum_scatter(partial_out, 'head', scatter_dimension=1, tiled=True)]
    unnamed x21 -> x32, local copies, waits for them, and re-layouts: 11.2 us -> 25.7 us
    ppermute x0 -> x7, starting transfers between devices: none -> 10.1 us  [per_device(): lax.ppermute(sent, 'req', [(i, (i + step) % size) for i in range(size)])]
    gather x0 -> x1, local copies, waits for them, and re-layouts: none -> 8.08 us  [per_device(): pieces = jnp.stack(gathered)[(place - jnp.arange(size)) % size]]
    squeeze x0 -> x1, local copies, waits for them, and re-layouts: none -> 6.27 us  [per_device(): sent = pieces[(place + step) % size]]
    all_to_all x1 -> x0, starting transfers between devices: 5.04 us -> none  [per_device(): lax.all_to_all(jnp.where(present[:, :, None, None], picked, jnp.zeros_lik...]
  transfers between devices with their start and end apart: 2 -> 8, of which waited for: 2 -> 3; matrix products, arithmetic and copies ran while one was open for 7% -> 10% of each run, Pallas kernels for 0% -> 0%
where the time goes in v1:
time: 493 us; the launch traced here: 490 us
  waiting for transfers between devices  226 us (46%)
  local copies, waits for them, and re-layouts  122 us (25%)
  matrix products  48.4 us (10%)
  other arithmetic  35.2 us (7%)
  loops' own time  22.8 us (5%)
  between operations  14.3 us (3%)
  blocking collectives  10.6 us (2%)
  starting transfers between devices  10.1 us (2%)
    reduce_scatter x1, waiting for transfers between devices, per_device(): lax.psum_scatter(partial_out, 'head', scatter_dimension=1, tiled=True)  148 us
    ppermute x7, waiting for transfers between devices, per_device(): lax.ppermute(sent, 'req', [(i, (i + step) % size) for i in range(size)])  77.4 us
    dynamic_update_slice x8, local copies, waits for them, and re-layouts, add_request(): return lax.dynamic_update_slice_in_dim(total, current + mixed, start, 0)  47.1 us
    dot_general x8, matrix products, add_request(): jnp.einsum('hwt,thd->whd', weights, cached[:, :, 1], preferred_element_ty...  27.4 us
    unnamed x32, local copies, waits for them, and re-layouts  25.7 us
    another operation x1, loops' own time, per_device(): attended = lax.fori_loop(0, owners.shape[0], add_request, attended)  22.8 us
    dot_general x1, matrix products, per_device(): jnp.dot(normed, w_in, preferred_element_type=jnp.float32)  15.4 us
    dynamic_slice x16, local copies, waits for them, and re-layouts, add_request(): cached = arrived[source, slot].reshape(-1, local_heads, 2, HD)  14.7 us
  transfers between devices with their start and end apart: 8, of which 3 were waited for; matrix products, arithmetic and copies ran while one was open for 10% of the time, Pallas kernels for 0%

profile of v1, /device:TPU:0, one launch (start us, length us, event | category | flops | bytes accessed | tf_op | source)
XLA Modules:
  0.0 490.0 jit_solution(10615824830760252706)
XLA Ops:
  6.6 1.3 dynamic-slice.11
  10.1 10.6 %all-reduce.2 = (s32[64]{0:T(128)S(1)}, s32[64]{0:T(128)S(1)}) all-reduce(s32[64]{0:T(128)S(1)} %bitcast_dynamic-update-slice_fusion.8, s32[64]{0:T(128)S(1)} %dynamic-update-slice.1), channel_id=2, replica_groups=mesh['groups'=2,'req'=8,'head'=2,'rep'=1] {'req'}, use_global_device_ids=true, to_apply=%add | all-reduce | flops 128 | bytes 1024
  21.6 8.0 %gather_fusion = bf16[8,512,1024]{2,1,0:T(8,128)(2,1)} fusion(bf16[8,512,1024]{2,1,0:T(8,128)(2,1)} %param.15, s32[1024]{0:T(1024)S(1)} %pad_clamp_fusion.1), kind=kCustom, calls=%fused_computation | custom fusion | bytes 16777248 | tf_op jit(solution)/shard_map/gather | solution.py:69
  29.7 7.2 %bitcast_select_fusion = bf16[8,1,512,1024]{3,2,1,0:T(8,128)(2,1)} fusion(bf16[8,512,1024]{2,1,0:T(8,128)(2,1)} %gather_fusion, pred[8]{0:T(512)(128)(4,1)S(1)} %broadcast_compare_fusion.1), kind=kLoop, calls=%fused_computation.26 | loop fusion | flops 4194304 | bytes 16777224 | tf_op jit(solution)/shard_map/jit(_where)/select_n | solution.py:70
  36.9 6.3 %constant_dynamic-slice_fusion.1 = (bf16[1,1,512,1024]{3,2,1,0:T(8,128)(2,1)}, bf16[1,1,512,1024]{3,2,1,0:T(8,128)(2,1)}, bf16[1,1,512,1024]{3,2,1,0:T(8,128)(2,...) fusion(bf16[8,1,512,1024]{3,2,1,0:T(8,128)(2,1)} %bitcast_selec, ...), kind=kLoop, calls=%fused_computation.61 | loop fusion | bytes 14680092 | tf_op jit(solution)/shard_map/squeeze | solution.py:75
  44.3 3.5 collective-permute-start.3
  48.5 1.4 fusion.15
  49.9 15.4 %multiply_convert_fusion = bf16[2048,2048]{0,1:T(8,128)(2,1)S(1)} fusion(bf16[1024,2048]{1,0:T(8,128)(2,1)} %param.16, bf16[2048,1024]{1,0:T(8,128)(2,1)S(1)} %copy-done.2, f32[2048]{0:T(1024)S(1)} %add_rsqrt_fusion.1, f32[2048]{0:T(1024)S(1)} %broadcast_multiply_fusion.1), kind=kOutput, calls=%fused_computation.19 | convolution fusion | flops 8619294720 | bytes 16793600 | tf_op jit(solution)/shard_map/dot_general | solution.py:81
  65.3 2.0 fusion.28
  67.3 1.8 copy-done.3
  69.2 2.5 copy.61
  71.7 3.0 copy.62
  74.7 2.8 fusion.20
  77.5 4.3 convert_multiply_fusion.1
  81.9 2.3 bitcast_dynamic-update-slice_fusion.7
  84.2 2.1 collective-permute-start.5
  86.2 2.3 bitcast_dynamic-update-slice_fusion.5
  88.6 3.4 collective-permute-start.6
  92.0 2.3 bitcast_dynamic-update-slice_fusion.4
  94.2 66.3 %collective-permute-done.2 = bf16[1,1,512,1024]{3,2,1,0:T(8,128)(2,1)} collective-permute-done((bf16[1,1,512,1024]{3,2,1,0:T(8,128)(2,1)}, bf16[1,1,512,1024]{3,2,1,0:T(8,128)(2,1)}, u32[]{:S(2)}, u32[]{:S(2)}) %collective-permute-start.2) | collective-permute-done | bytes 1048608 | tf_op jit(solution)/shard_map/ppermute | solution.py:76
  160.5 2.3 bitcast_dynamic-update-slice_fusion.3
  162.8 2.3 bitcast_dynamic-update-slice_fusion.2
  165.1 2.3 bitcast_dynamic-update-slice_fusion.1
  168.5 11.1 %collective-permute-done.6 = bf16[1,1,512,1024]{3,2,1,0:T(8,128)(2,1)S(1)} collective-permute-done((bf16[1,1,512,1024]{3,2,1,0:T(8,128)(2,1)S(1)}, bf16[1,1,512,1024]{3,2,1,0:T(8,128)(2,1)S(1)}, u32[]{:S(2)}, u32[]{:S(2)}) %collective-permute-start.6) | collective-permute-done | bytes 1048608 | tf_op jit(solution)/shard_map/ppermute | solution.py:76
  180.6 8.1 %gather_fusion.1 = bf16[8,512,1024]{2,1,0:T(8,128)(2,1)} fusion(bf16[8,512,1024]{2,1,0:T(8,128)(2,1)} %bitcast.25, s32[1024]{0:T(1024)S(1)} %pad_clamp_fusion), kind=kCustom, calls=%fused_computation.1 | custom fusion | bytes 16777248 | tf_op jit(solution)/shard_map/gather | solution.py:77
  188.7 127.0 %while.14 = (s32[]{:T(128)}, f32[2048,4,128]{0,2,1:T(8,128)}, s32[2048]{0:T(1024)S(1)}, s32[8]{0:T(128)S(1)}, bf16[8,1,512,1024]{3,2,0,1:T(8,128)(2,1)}, /*index...) while((s32[]{:T(128)}, f32[2048,4,128]{0,2,1:T(8,128)}, ...), condition=%wide.region_8.9_spmd.clone, body=%wide.region_6.8_spmd.clone.sunk | while | flops 544742400 | bytes 9975023 | solution.py:119
  195.3 3.4 fusion.36
  198.8 5.8 %dynamic_update_slice.9 = f32[2048,4,128]{0,2,1:T(8,128)} dynamic-update-slice(f32[2048,4,128]{0,2,1:T(8,128)} %get-tuple-element.275, f32[512,4,128]{0,2,1:T(8,128)S(1)} %fusion.36, s32[]{:T(128)S(6)} %min.10, s32[]{:T(128)} %constant.141.clone.1..sunk, s32[]{:T(128)} %constant.141.clone.1..sunk) | dynamic-update-slice | bytes 2097156 | tf_op jit(solution)/shard_map/while/body/eval_jaxpr/dynamic_update_slice | solution.py:117
  211.1 3.4 fusion.36
  214.5 6.3 %dynamic_update_slice.9 = f32[2048,4,128]{0,2,1:T(8,128)} dynamic-update-slice(f32[2048,4,128]{0,2,1:T(8,128)} %get-tuple-element.275, f32[512,4,128]{0,2,1:T(8,128)S(1)} %fusion.36, s32[]{:T(128)S(6)} %min.10, s32[]{:T(128)} %constant.141.clone.1..sunk, s32[]{:T(128)} %constant.141.clone.1..sunk) | dynamic-update-slice | bytes 2097156 | tf_op jit(solution)/shard_map/while/body/eval_jaxpr/dynamic_update_slice | solution.py:117
  227.4 3.4 fusion.36
  230.8 6.3 %dynamic_update_slice.9 = f32[2048,4,128]{0,2,1:T(8,128)} dynamic-update-slice(f32[2048,4,128]{0,2,1:T(8,128)} %get-tuple-element.275, f32[512,4,128]{0,2,1:T(8,128)S(1)} %fusion.36, s32[]{:T(128)S(6)} %min.10, s32[]{:T(128)} %constant.141.clone.1..sunk, s32[]{:T(128)} %constant.141.clone.1..sunk) | dynamic-update-slice | bytes 2097156 | tf_op jit(solution)/shard_map/while/body/eval_jaxpr/dynamic_update_slice | solution.py:117
  243.7 3.4 fusion.36
  247.1 6.3 %dynamic_update_slice.9 = f32[2048,4,128]{0,2,1:T(8,128)} dynamic-update-slice(f32[2048,4,128]{0,2,1:T(8,128)} %get-tuple-element.275, f32[512,4,128]{0,2,1:T(8,128)S(1)} %fusion.36, s32[]{:T(128)S(6)} %min.10, s32[]{:T(128)} %constant.141.clone.1..sunk, s32[]{:T(128)} %constant.141.clone.1..sunk) | dynamic-update-slice | bytes 2097156 | tf_op jit(solution)/shard_map/while/body/eval_jaxpr/dynamic_update_slice | solution.py:117
  259.9 3.4 fusion.36
  263.4 6.3 %dynamic_update_slice.9 = f32[2048,4,128]{0,2,1:T(8,128)} dynamic-update-slice(f32[2048,4,128]{0,2,1:T(8,128)} %get-tuple-element.275, f32[512,4,128]{0,2,1:T(8,128)S(1)} %fusion.36, s32[]{:T(128)S(6)} %min.10, s32[]{:T(128)} %constant.141.clone.1..sunk, s32[]{:T(128)} %constant.141.clone.1..sunk) | dynamic-update-slice | bytes 2097156 | tf_op jit(solution)/shard_map/while/body/eval_jaxpr/dynamic_update_slice | solution.py:117
  276.2 3.4 fusion.36
  279.7 6.3 %dynamic_update_slice.9 = f32[2048,4,128]{0,2,1:T(8,128)} dynamic-update-slice(f32[2048,4,128]{0,2,1:T(8,128)} %get-tuple-element.275, f32[512,4,128]{0,2,1:T(8,128)S(1)} %fusion.36, s32[]{:T(128)S(6)} %min.10, s32[]{:T(128)} %constant.141.clone.1..sunk, s32[]{:T(128)} %constant.141.clone.1..sunk) | dynamic-update-slice | bytes 2097156 | tf_op jit(solution)/shard_map/while/body/eval_jaxpr/dynamic_update_slice | solution.py:117
  292.5 3.4 fusion.36
  295.8 5.0 %dynamic_update_slice.9 = f32[2048,4,128]{0,2,1:T(8,128)} dynamic-update-slice(f32[2048,4,128]{0,2,1:T(8,128)} %get-tuple-element.275, f32[512,4,128]{0,2,1:T(8,128)S(1)} %fusion.36, s32[]{:T(128)S(6)} %min.10, s32[]{:T(128)} %constant.141.clone.1..sunk, s32[]{:T(128)} %constant.141.clone.1..sunk) | dynamic-update-slice | bytes 2097156 | tf_op jit(solution)/shard_map/while/body/eval_jaxpr/dynamic_update_slice | solution.py:117
  307.4 3.3 fusion.36
  310.7 5.0 %dynamic_update_slice.9 = f32[2048,4,128]{0,2,1:T(8,128)} dynamic-update-slice(f32[2048,4,128]{0,2,1:T(8,128)} %get-tuple-element.275, f32[512,4,128]{0,2,1:T(8,128)S(1)} %fusion.36, s32[]{:T(128)S(6)} %min.10, s32[]{:T(128)} %constant.141.clone.1..sunk, s32[]{:T(128)} %constant.141.clone.1..sunk) | dynamic-update-slice | bytes 2097156 | tf_op jit(solution)/shard_map/while/body/eval_jaxpr/dynamic_update_slice | solution.py:117
  315.7 2.5 reduce_sum.98
  318.2 2.9 multiply_reduce_fusion
  321.6 2.4 fusion.19
  324.1 5.6 %fusion.29 = f32[2048,1024]{1,0:T(8,128)} fusion(bf16[2048,512]{0,1:T(8,128)(2,1)S(1)} %bitcast.103, bf16[512,1024]{1,0:T(8,128)(2,1)S(1)} %copy-done), kind=kOutput, calls=%fused_computation.78 | convolution fusion | flops 2147483648 | bytes 11534336 | tf_op jit(solution)/shard_map/dot_general | solution.py:125
  329.7 148.5 %reduce-scatter.2.cloned.1.call-done = f32[2048,512]{1,0:T(8,128)} async-done(((f32[2048,1024]{1,0:T(8,128)}), f32[2048,512]{1,0:T(8,128)}) %reduce-scatter.2.cloned.1.call-update) | async-done | bytes 4194320 | tf_op jit(solution)/shard_map/reduce_scatter | solution.py:126
  478.2 4.9 %add_convert_fusion = bf16[2048,512]{1,0:T(8,128)(2,1)} fusion(f32[2048,512]{1,0:T(8,128)} %reduce-scatter.2.cloned.1.call-done, bf16[2048,1024]{1,0:T(8,128)(2,1)} %param.10, s32[]{:T(128)S(6)} %select_n.166), kind=kLoop, calls=%fused_computation.33 | loop fusion | flops 3145728 | bytes 8388612 | tf_op jit(solution)/shard_map/convert_element_type | solution.py:131
  (100 shorter events, 36.6 us)
Async XLA Ops:
  6.5 317.6 %copy-start = (bf16[512,1024]{1,0:T(8,128)(2,1)S(1)}, bf16[512,1024]{1,0:T(8,128)(2,1)}, u32[]{:S(2)}) copy-start(bf16[512,1024]{1,0:T(8,128)(2,1)} %param.17) | copy-start | bytes 3145732
  6.5 471.7 %reduce-scatter.2.cloned.1.call-start = ((), (), s32[]{:S(2)}) async-start(), calls=%async_computation.1 | async-start | bytes 12582912 | tf_op jit(solution)/shard_map/reduce_scatter | solution.py:126
  36.9 11.0 %copy-start.2 = (bf16[2048,1024]{1,0:T(8,128)(2,1)S(1)}, bf16[2048,1024]{1,0:T(8,128)(2,1)}, u32[]{:S(2)}) copy-start(bf16[2048,1024]{1,0:T(8,128)(2,1)} %param.10) | copy-start | bytes 12582916
  43.1 41.0 %collective-permute-start = (bf16[1,1,512,1024]{3,2,1,0:T(8,128)(2,1)}, bf16[1,1,512,1024]{3,2,1,0:T(8,128)(2,1)}, u32[]{:S(2)}, u32[]{:S(2)}) collective-permute-start(bf16[1,1,512,1024]{3,2,1,0:T(8,128)(2,1)} %get-tuple-element.212), channel_id=1, source_target_pairs={{0,2},{2,4},{4,6},{6,8},{8,10},{10,12},{12,14},{14,0},{1,3},{3,5},... | collective-permute-start | bytes 3145736 | tf_op jit(solution)/shard_map/ppermute | solution.py:76
  43.1 45.4 %collective-permute-start.1 = (bf16[1,1,512,1024]{3,2,1,0:T(8,128)(2,1)}, bf16[1,1,512,1024]{3,2,1,0:T(8,128)(2,1)}, u32[]{:S(2)}, u32[]{:S(2)}) collective-permute-start(bf16[1,1,512,1024]{3,2,1,0:T(8,128)(2,1)} %get-tuple-element.211), channel_id=1, source_target_pairs={{0,4},{2,6},{4,8},{6,10},{8,12},{10,14},{12,0},{14,2},{1,5},{3,7},... | collective-permute-start | bytes 3145736 | tf_op jit(solution)/shard_map/ppermute | solution.py:76
  44.0 116.5 %collective-permute-start.2 = (bf16[1,1,512,1024]{3,2,1,0:T(8,128)(2,1)}, bf16[1,1,512,1024]{3,2,1,0:T(8,128)(2,1)}, u32[]{:S(2)}, u32[]{:S(2)}) collective-permute-start(bf16[1,1,512,1024]{3,2,1,0:T(8,128)(2,1)} %get-tuple-element.210), channel_id=1, source_target_pairs={{0,6},{2,8},{4,10},{6,12},{8,14},{10,0},{12,2},{14,4},{1,7},{3,9},... | collective-permute-start | bytes 3145736 | tf_op jit(solution)/shard_map/ppermute | solution.py:76
  44.3 118.5 %collective-permute-start.3 = (bf16[1,1,512,1024]{3,2,1,0:T(8,128)(2,1)}, bf16[1,1,512,1024]{3,2,1,0:T(8,128)(2,1)}, u32[]{:S(2)}, u32[]{:S(2)}) collective-permute-start(bf16[1,1,512,1024]{3,2,1,0:T(8,128)(2,1)} %get-tuple-element.209), channel_id=1, source_target_pairs={{0,8},{2,10},{4,12},{6,14},{8,0},{10,2},{12,4},{14,6},{1,9},{3,11}... | collective-permute-start | bytes 3145736 | tf_op jit(solution)/shard_map/ppermute | solution.py:76
  47.8 117.3 %collective-permute-start.4 = (bf16[1,1,512,1024]{3,2,1,0:T(8,128)(2,1)}, bf16[1,1,512,1024]{3,2,1,0:T(8,128)(2,1)}, u32[]{:S(2)}, u32[]{:S(2)}) collective-permute-start(bf16[1,1,512,1024]{3,2,1,0:T(8,128)(2,1)} %get-tuple-element.208), channel_id=1, source_target_pairs={{0,10},{2,12},{4,14},{6,0},{8,2},{10,4},{12,6},{14,8},{1,11},{3,13... | collective-permute-start | bytes 3145736 | tf_op jit(solution)/shard_map/ppermute | solution.py:76
  65.3 3.8 copy-start.3
  77.5 6.6 %copy-start.5 = (bf16[1,1,512,1024]{3,2,1,0:T(8,128)(2,1)S(1)}, bf16[1,1,512,1024]{3,2,1,0:T(8,128)(2,1)}, u32[]{:S(2)}) copy-start(bf16[1,1,512,1024]{3,2,1,0:T(8,128)(2,1)} %get-tuple-element.207) | copy-start | bytes 3145732
  77.5 11.0 %copy-start.4 = (bf16[1,1,512,1024]{3,2,1,0:T(8,128)(2,1)S(1)}, bf16[1,1,512,1024]{3,2,1,0:T(8,128)(2,1)}, u32[]{:S(2)}) copy-start(bf16[1,1,512,1024]{3,2,1,0:T(8,128)(2,1)} %get-tuple-element.206) | copy-start | bytes 3145732
  84.2 83.2 %collective-permute-start.5 = (bf16[1,1,512,1024]{3,2,1,0:T(8,128)(2,1)S(1)}, bf16[1,1,512,1024]{3,2,1,0:T(8,128)(2,1)S(1)}, u32[]{:S(2)}, u32[]{:S(2)}) collective-permute-start(bf16[1,1,512,1024]{3,2,1,0:T(8,128)(2,1)S(1)} %copy-done.5), channel_id=1, source_target_pairs={{0,12},{2,14},{4,0},{6,2},{8,4},{10,6},{12,8},{14,10},{1,13},{3,15... | collective-permute-start | bytes 3145736 | tf_op jit(solution)/shard_map/ppermute | solution.py:76
  88.6 91.0 %collective-permute-start.6 = (bf16[1,1,512,1024]{3,2,1,0:T(8,128)(2,1)S(1)}, bf16[1,1,512,1024]{3,2,1,0:T(8,128)(2,1)S(1)}, u32[]{:S(2)}, u32[]{:S(2)}) collective-permute-start(bf16[1,1,512,1024]{3,2,1,0:T(8,128)(2,1)S(1)} %copy-done.4), channel_id=1, source_target_pairs={{0,14},{2,0},{4,2},{6,4},{8,6},{10,8},{12,10},{14,12},{1,15},{3,1}... | collective-permute-start | bytes 3145736 | tf_op jit(solution)/shard_map/ppermute | solution.py:76
  180.6 8.1 %copy-start.6 = (s32[1,2048]{1,0:T(1,128)S(1)}, s32[1,2048]{1,0:T(1,128)}, u32[]{:S(2)}) copy-start(s32[1,2048]{1,0:T(1,128)} %param.11) | copy-start | bytes 24580
  180.6 8.1 %copy-start.7 = (s32[8,1]{0,1:T(1,128)S(1)}, s32[8,1]{0,1:T(1,128)}, u32[]{:S(2)}) copy-start(s32[8,1]{0,1:T(1,128)} %param.12) | copy-start | bytes 100
  180.6 8.1 %copy-start.8 = (s32[1,8]{1,0:T(1,128)S(1)}, s32[1,8]{1,0:T(1,128)}, u32[]{:S(2)}) copy-start(s32[1,8]{1,0:T(1,128)} %param.14) | copy-start | bytes 100
  318.2 3.5 copy-start.1
Sparse Core Ops, SparseCore 0:
  329.9 148.3 reduce-scatter.1
